TPU v7x, 32 devices: a whole 2x2x4 slice. The times are simulated.
32 devices in a mesh: blk: 8 (over z, x), uly: 4 (over y, core).
Axes of the slice: x: 2, y: 2, z: 4, core: 2. Of those that a mesh axis runs over, the one named last changes fastest.
Arguments:
- query_projection: bfloat16 [4096, 4096], P(('blk', 'uly')), may hold values from -4.5 to 4.5
- key_projection: bfloat16 [4096, 512], P(('blk', 'uly')), may hold values from -4.5 to 4.5
- value_projection: bfloat16 [4096, 512], P(('blk', 'uly')), may hold values from -6 to 6
- doc_start: int32 [4096], P('blk'), may hold values from 0 to 4095, as said below
Outputs:
- attn: bfloat16 [4096, 4096], P(('blk', 'uly'))
Inputs may be any that keep to these rules, and one draw needn't show every extreme that they name: Documents are contiguous runs of positions: doc_start[0] = 0, doc_start never falls, doc_start[i] <= i, and doc_start[doc_start[i]] = doc_start[i]. Every document has at most 1024 positions; the first has exactly 1024, and another of exactly 1024 begins strictly inside a block of 512 positions. The last position begins a document of its own.
All inputs are finite; a program needn't handle non-finite values.
Results may differ from a plain program's by a relative error of at most 0.0031.
Values may be sent and summed in bfloat16 or wider, within the bound.
A program may use at most 64 MiB of HBM per device.

v0:
```python
import jax
import jax.numpy as jnp
from jax import lax
from jax.sharding import PartitionSpec as P

HEAD_WIDTH = 128
CYCLE_STEPS = 2
POSITION_GROUP = 512
masked_score = -1e30


def from_behind(block, axis, distance):
    devices = range(lax.axis_size(axis))
    route = [(i - distance, i) for i in devices if i - distance in devices]
    return lax.ppermute(block, axis, route)


def local(query_projection, key_projection, value_projection, doc_start):
    width = lax.axis_size("uly")
    tokens_dev = query_projection.shape[0]
    kv_heads = key_projection.shape[1] // HEAD_WIDTH
    repeats = max(1, width // kv_heads)

    def widen_heads(source):
        split_heads = source.reshape(tokens_dev, kv_heads, 1, HEAD_WIDTH)
        copies = jnp.broadcast_to(split_heads, (tokens_dev, kv_heads, repeats, HEAD_WIDTH))
        return copies.reshape(tokens_dev, kv_heads * repeats * HEAD_WIDTH)

    query_rows = lax.all_to_all(query_projection, "uly", split_axis=1, concat_axis=0, tiled=True)
    key_rows, value_rows = (
        lax.all_to_all(widen_heads(key_projection), "uly", split_axis=1, concat_axis=0, tiled=True),
        lax.all_to_all(
            widen_heads(value_projection), "uly", split_axis=1, concat_axis=0, tiled=True
        ),
    )
    row_count = query_rows.shape[0]
    local_kv = key_rows.shape[1] // HEAD_WIDTH
    local_q = query_rows.shape[1] // HEAD_WIDTH
    query_group_width = local_q // local_kv
    earlier = []
    for step in range(CYCLE_STEPS):
        earlier.insert(0, from_behind((key_rows, value_rows), "blk", step + 1))
    joined_keys = jnp.concatenate([piece[0] for piece in earlier] + [key_rows], axis=0).reshape(
        -1, local_kv, HEAD_WIDTH
    )
    joined_values = jnp.concatenate([piece[1] for piece in earlier] + [value_rows], axis=0).reshape(
        -1, local_kv, HEAD_WIDTH
    )
    lead = CYCLE_STEPS * row_count
    base = lax.axis_index("blk") * row_count
    anchor = base - lead
    query_heads = query_rows.reshape(row_count, local_kv, query_group_width, HEAD_WIDTH)
    score_scale = HEAD_WIDTH ** (-0.5)

    def one_tile(index):
        start = index * POSITION_GROUP
        query_tile = lax.dynamic_slice_in_dim(query_heads, start, POSITION_GROUP, 0)
        starts = lax.dynamic_slice_in_dim(doc_start, start, POSITION_GROUP, 0)
        query_places = base + start + jnp.arange(POSITION_GROUP, dtype=jnp.int32)
        first_tile = (jnp.min(starts) - anchor) // POSITION_GROUP
        last_tile = (lead + start) // POSITION_GROUP

        def add_tile(tile, carry):
            running_maximum, running_sum, running_output = carry
            key_start = tile * POSITION_GROUP
            key_tile = lax.dynamic_slice_in_dim(joined_keys, key_start, POSITION_GROUP, 0)
            value_tile = lax.dynamic_slice_in_dim(joined_values, key_start, POSITION_GROUP, 0)
            key_places = anchor + key_start + jnp.arange(POSITION_GROUP, dtype=jnp.int32)
            seen = (key_places[None, :] >= starts[:, None]) & (
                key_places[None, :] <= query_places[:, None]
            )
            seen = seen[:, None, None, :]
            scores = (
                jnp.einsum(
                    "tkgd,nkd->tkgn", query_tile, key_tile, preferred_element_type=jnp.float32
                )
                * score_scale
            )
            masked = jnp.where(seen, scores, masked_score)
            fresh = jnp.maximum(running_maximum, jnp.max(masked, axis=-1))
            factor = jnp.exp(running_maximum - fresh)
            exps = jnp.where(seen, jnp.exp(masked - fresh[..., None]), 0.0)
            running_sum = running_sum * factor + jnp.sum(exps, axis=-1)
            blended = jnp.einsum(
                "tkgn,nkd->tkgd",
                exps.astype(jnp.bfloat16),
                value_tile,
                preferred_element_type=jnp.float32,
            )
            running_output = running_output * factor[..., None] + blended
            return (fresh, running_sum, running_output)

        running_maximum = jnp.full(
            (POSITION_GROUP, local_kv, query_group_width), masked_score, jnp.float32
        )
        running_sum = jnp.zeros((POSITION_GROUP, local_kv, query_group_width), jnp.float32)
        running_output = jnp.zeros(
            (POSITION_GROUP, local_kv, query_group_width, HEAD_WIDTH), jnp.float32
        )
        running_maximum, running_sum, running_output = lax.fori_loop(
            first_tile, last_tile + 1, add_tile, (running_maximum, running_sum, running_output)
        )
        return (running_output / running_sum[..., None]).astype(jnp.bfloat16)

    outputs = lax.map(one_tile, jnp.arange(row_count // POSITION_GROUP, dtype=jnp.int32))
    attn = outputs.reshape(row_count, local_q * HEAD_WIDTH)
    return lax.all_to_all(attn, "uly", split_axis=0, concat_axis=1, tiled=True)


def solution(mesh):
    placed = (P(("blk", "uly"), None), P(("blk", "uly"), None), P(("blk", "uly"), None), P("blk"))
    return jax.shard_map(
        local, mesh=mesh, in_specs=placed, out_specs=P(("blk", "uly"), None), check_vma=False
    )
```

profile of v0, /device:TPU:18, one launch (start us, length us, event | category | flops | bytes accessed | tf_op | source)
XLA Modules:
  0.0 90.7 jit_solution(1253593889368224903)
XLA Ops:
  0.0 1.7 %copy.24 = bf16[128,512]{0,1:T(8,128)(2,1)} copy(bf16[128,512]{1,0:T(8,128)(2,1)} %param.8) | data formatting | bytes 262144 | tf_op args[2]
  1.7 3.3 %all-to-all-start.2 = ((bf16[128,4,128]{0,2,1:T(8,128)(2,1)}), bf16[128,4,128]{0,2,1:T(8,128)(2,1)S(1)}, u32[]{:S(2)}, u32[]{:S(2)}) async-start(bf16[128,4,128]{0,2,1:T(8,128)(2,1)} %bitcast.5), calls=%async_computation.2 | async-start | bytes 262144 | tf_op jit(solution)/shard_map/all_to_all | solution.py:32
  5.7 3.9 %all-to-all-done.2 = bf16[128,4,128]{0,2,1:T(8,128)(2,1)S(1)} async-done(((bf16[128,4,128]{0,2,1:T(8,128)(2,1)}), bf16[128,4,128]{0,2,1:T(8,128)(2,1)S(1)}, u32[]{:S(2)}, u32[]{:S(2)}) %all-to-all-start.2) | async-done | bytes 131104 | tf_op jit(solution)/shard_map/all_to_all | solution.py:32
  9.6 3.3 %all-to-all-start = ((bf16[128,4,128]{2,0,1:T(8,128)(2,1)}), bf16[128,4,128]{2,0,1:T(8,128)(2,1)S(1)}, u32[]{:S(2)}, u32[]{:S(2)}) async-start(bf16[128,4,128]{2,0,1:T(8,128)(2,1)} %copy_bitcast_fusion.1), calls=%async_computation | async-start | bytes 262144 | tf_op jit(solution)/shard_map/all_to_all | solution.py:31
  12.9 2.3 %copy.39 = bf16[16,4,8,1024]{3,2,0,1:T(8,128)(2,1)} copy(bf16[16,4,8,1024]{3,2,1,0:T(8,128)(2,1)} %bitcast.111) | data formatting | bytes 2097152 | tf_op jit(solution)/shard_map/all_to_all | solution.py:29
  15.2 2.3 %all-to-all-done = bf16[128,4,128]{2,0,1:T(8,128)(2,1)S(1)} async-done(((bf16[128,4,128]{2,0,1:T(8,128)(2,1)}), bf16[128,4,128]{2,0,1:T(8,128)(2,1)S(1)}, u32[]{:S(2)}, u32[]{:S(2)}) %all-to-all-start) | async-done | bytes 131104 | tf_op jit(solution)/shard_map/all_to_all | solution.py:31
  17.5 3.5 %all-to-all-start.1 = ((bf16[128,4,1024]{2,0,1:T(8,128)(2,1)}), bf16[128,4,1024]{2,0,1:T(8,128)(2,1)S(1)}, u32[]{:S(2)}, u32[]{:S(2)}) async-start(bf16[128,4,1024]{2,0,1:T(8,128)(2,1)} %bitcast.83), calls=%async_computation.1 | async-start | bytes 2097152 | tf_op jit(solution)/shard_map/all_to_all | solution.py:29
  21.2 3.5 %collective-permute-start.2 = (bf16[512,128]{1,0:T(8,128)(2,1)S(1)}, bf16[512,128]{1,0:T(8,128)(2,1)S(1)}, u32[]{:S(2)}, u32[]{:S(2)}) collective-permute-start(bf16[512,128]{1,0:T(8,128)(2,1)S(1)} %bitcast.116), channel_id=1, source_target_pairs={{0,8},{4,12},{8,16},{12,20},{16,24},{20,28},{1,9},{5,13},{9,17},{1... | collective-permute-start | bytes 393224 | tf_op jit(solution)/shard_map/ppermute | solution.py:15
  24.7 1.9 %collective-permute-start.3 = (bf16[512,128]{1,0:T(8,128)(2,1)S(1)}, bf16[512,128]{1,0:T(8,128)(2,1)S(1)}, u32[]{:S(2)}, u32[]{:S(2)}) collective-permute-start(bf16[512,128]{1,0:T(8,128)(2,1)S(1)} %bitcast.117), channel_id=1, source_target_pairs={{0,4},{4,8},{8,12},{12,16},{16,20},{20,24},{24,28},{1,5},{5,9},{9,... | collective-permute-start | bytes 393224 | tf_op jit(solution)/shard_map/ppermute | solution.py:15
  26.6 1.4 %reduce_min.10 = s32[]{:T(128)} reduce(s32[512]{0:T(512)} %param.9, s32[]{:T(128)} %constant.93.clone.1), dimensions={0}, to_apply=%region_0.1 | reduce | flops 511 | bytes 2056 | tf_op jit(solution)/shard_map/while/body/eval_jaxpr/reduce_min | solution.py:60
  28.7 1.9 %collective-permute-start = (bf16[512,128]{1,0:T(8,128)(2,1)S(1)}, bf16[512,128]{1,0:T(8,128)(2,1)S(1)}, u32[]{:S(2)}, u32[]{:S(2)}) collective-permute-start(bf16[512,128]{1,0:T(8,128)(2,1)S(1)} %bitcast.113), channel_id=1, source_target_pairs={{0,8},{4,12},{8,16},{12,20},{16,24},{20,28},{1,9},{5,13},{9,17},{1... | collective-permute-start | bytes 393224 | tf_op jit(solution)/shard_map/ppermute | solution.py:15
  30.6 2.1 %collective-permute-start.1 = (bf16[512,128]{1,0:T(8,128)(2,1)S(1)}, bf16[512,128]{1,0:T(8,128)(2,1)S(1)}, u32[]{:S(2)}, u32[]{:S(2)}) collective-permute-start(bf16[512,128]{1,0:T(8,128)(2,1)S(1)} %bitcast.114), channel_id=1, source_target_pairs={{0,4},{4,8},{8,12},{12,16},{16,20},{20,24},{24,28},{1,5},{5,9},{9,... | collective-permute-start | bytes 393224 | tf_op jit(solution)/shard_map/ppermute | solution.py:15
  32.8 0.8 maximum_bitcast_fusion.1
  33.5 2.6 %collective-permute-done = bf16[512,128]{1,0:T(8,128)(2,1)S(1)} collective-permute-done((bf16[512,128]{1,0:T(8,128)(2,1)S(1)}, bf16[512,128]{1,0:T(8,128)(2,1)S(1)}, u32[]{:S(2)}, u32[]{:S(2)}) %collective-permute-start) | collective-permute-done | bytes 131104 | tf_op jit(solution)/shard_map/ppermute | solution.py:15
  36.2 1.9 %collective-permute-done.1 = bf16[512,128]{1,0:T(8,128)(2,1)S(1)} collective-permute-done((bf16[512,128]{1,0:T(8,128)(2,1)S(1)}, bf16[512,128]{1,0:T(8,128)(2,1)S(1)}, u32[]{:S(2)}, u32[]{:S(2)}) %collective-permute-start.1) | collective-permute-done | bytes 131104 | tf_op jit(solution)/shard_map/ppermute | solution.py:15
  38.1 0.8 maximum_bitcast_fusion
  40.2 29.5 %while.24 = (s32[]{:T(128)}, f32[512,1,8]{0,2,1:T(8,128)S(1)}, f32[512,1,8]{0,2,1:T(8,128)}, f32[512,1,8,128]{0,3,2,1:T(8,128)S(1)}, s32[]{:T(128)}, /*index=5*/...) while((s32[]{:T(128)}, f32[512,1,8]{0,2,1:T(8,128)S(1)}, ...), condition=%wide.region_4.5_spmd.clone, body=%wide.region_1.4_spmd.clone.sunk | while | flops 1102853120 | bytes 32123144 | solution.py:100
  40.2 0.9 %compare_and_fusion.2 = pred[512,512]{0,1:T(8,128)(4,1)S(1)} fusion(s32[512]{0:T(512)S(1)} %get-tuple-element.256, s32[512]{0:T(512)} %get-tuple-element.295, s32[512]{0:T(512)S(1)} %get-tuple-element.257), kind=kLoop, calls=%fused_computation.12.clone.1 | loop fusion | flops 786432 | bytes 268288 | tf_op jit(solution)/shard_map/while/body/eval_jaxpr/while/body/and | solution.py:69
  41.1 2.4 %fusion.31 = (f32[512,8]{0,1:T(8,128)S(1)}, f32[512,512,8]{1,0,2:T(8,128)S(1)}) fusion(pred[512,512]{0,1:T(8,128)(4,1)S(1)} %compare_and_fusion.2, bf16[512,1,8,128]{3,0,2,1:T(8,128)(2,1)S(1)} %get-tuple-element.297, bf16[1536,1,128]{2,0,1:T(8,128)(2,1)} %get-tuple-element.296, s32[]{:T(128)S(6)} %select_n.64), kind=kOutput, calls=%fused_computation.3.clone.1 | convolution fusion | flops 543158272 | bytes 9846788 | tf_op jit(solution)/shard_map/while/body/eval_jaxpr/while/body/tkgd,nkd->tkgn/dot_general | solution.py:74
  43.6 3.7 %bitcast_add_fusion.5 = f32[512,1,8,128]{0,3,2,1:T(8,128)S(1)} fusion(f32[512,1,8,128]{0,3,2,1:T(8,128)S(1)} %get-tuple-element.279, f32[512,512,8]{1,0,2:T(8,128)S(1)} %get-tuple-element.260, f32[512,8]{0,1:T(8,128)S(1)} %bitcast.106, pred[512,512]{0,1:T(8,128)(4,1)S(1)} %compare_and_fusion.2, f32[512,8]{0,1:T(8,128)S(1)} %get-tuple-element.261, ...), kind=kOutput, calls=%fused_computation.9.clone.1 | convolution fusion | flops 548405248 | bytes 13008900 | tf_op jit(solution)/shard_map/while/body/eval_jaxpr/while/body/tkgn,nkd->tkgd/dot_general | solution.py:84
  47.3 2.0 %fusion.33 = f32[512,8]{0,1:T(8,128)S(1)} fusion(f32[512,512,8]{1,0,2:T(8,128)S(1)} %get-tuple-element.260, f32[512,8]{0,1:T(8,128)S(1)} %bitcast.107, pred[512,512]{0,1:T(8,128)(4,1)S(1)} %compare_and_fusion.2), kind=kLoop, calls=%fused_computation.5.clone.1 | loop fusion | flops 10481664 | bytes 8683520 | tf_op jit(solution)/shard_map/while/body/eval_jaxpr/while/body/reduce_sum | solution.py:83
  50.0 0.9 %compare_and_fusion.2 = pred[512,512]{0,1:T(8,128)(4,1)S(1)} fusion(s32[512]{0:T(512)S(1)} %get-tuple-element.256, s32[512]{0:T(512)} %get-tuple-element.295, s32[512]{0:T(512)S(1)} %get-tuple-element.257), kind=kLoop, calls=%fused_computation.12.clone.1 | loop fusion | flops 786432 | bytes 268288 | tf_op jit(solution)/shard_map/while/body/eval_jaxpr/while/body/and | solution.py:69
  51.0 2.4 %fusion.31 = (f32[512,8]{0,1:T(8,128)S(1)}, f32[512,512,8]{1,0,2:T(8,128)S(1)}) fusion(pred[512,512]{0,1:T(8,128)(4,1)S(1)} %compare_and_fusion.2, bf16[512,1,8,128]{3,0,2,1:T(8,128)(2,1)S(1)} %get-tuple-element.297, bf16[1536,1,128]{2,0,1:T(8,128)(2,1)} %get-tuple-element.296, s32[]{:T(128)S(6)} %select_n.64), kind=kOutput, calls=%fused_computation.3.clone.1 | convolution fusion | flops 543158272 | bytes 9846788 | tf_op jit(solution)/shard_map/while/body/eval_jaxpr/while/body/tkgd,nkd->tkgn/dot_general | solution.py:74
  53.4 3.7 %bitcast_add_fusion.5 = f32[512,1,8,128]{0,3,2,1:T(8,128)S(1)} fusion(f32[512,1,8,128]{0,3,2,1:T(8,128)S(1)} %get-tuple-element.279, f32[512,512,8]{1,0,2:T(8,128)S(1)} %get-tuple-element.260, f32[512,8]{0,1:T(8,128)S(1)} %bitcast.106, pred[512,512]{0,1:T(8,128)(4,1)S(1)} %compare_and_fusion.2, f32[512,8]{0,1:T(8,128)S(1)} %get-tuple-element.261, ...), kind=kOutput, calls=%fused_computation.9.clone.1 | convolution fusion | flops 548405248 | bytes 13008900 | tf_op jit(solution)/shard_map/while/body/eval_jaxpr/while/body/tkgn,nkd->tkgd/dot_general | solution.py:84
  57.1 2.0 %fusion.33 = f32[512,8]{0,1:T(8,128)S(1)} fusion(f32[512,512,8]{1,0,2:T(8,128)S(1)} %get-tuple-element.260, f32[512,8]{0,1:T(8,128)S(1)} %bitcast.107, pred[512,512]{0,1:T(8,128)(4,1)S(1)} %compare_and_fusion.2), kind=kLoop, calls=%fused_computation.5.clone.1 | loop fusion | flops 10481664 | bytes 8683520 | tf_op jit(solution)/shard_map/while/body/eval_jaxpr/while/body/reduce_sum | solution.py:83
  59.8 0.9 %compare_and_fusion.2 = pred[512,512]{0,1:T(8,128)(4,1)S(1)} fusion(s32[512]{0:T(512)S(1)} %get-tuple-element.256, s32[512]{0:T(512)} %get-tuple-element.295, s32[512]{0:T(512)S(1)} %get-tuple-element.257), kind=kLoop, calls=%fused_computation.12.clone.1 | loop fusion | flops 786432 | bytes 268288 | tf_op jit(solution)/shard_map/while/body/eval_jaxpr/while/body/and | solution.py:69
  60.8 2.4 %fusion.31 = (f32[512,8]{0,1:T(8,128)S(1)}, f32[512,512,8]{1,0,2:T(8,128)S(1)}) fusion(pred[512,512]{0,1:T(8,128)(4,1)S(1)} %compare_and_fusion.2, bf16[512,1,8,128]{3,0,2,1:T(8,128)(2,1)S(1)} %get-tuple-element.297, bf16[1536,1,128]{2,0,1:T(8,128)(2,1)} %get-tuple-element.296, s32[]{:T(128)S(6)} %select_n.64), kind=kOutput, calls=%fused_computation.3.clone.1 | convolution fusion | flops 543158272 | bytes 9846788 | tf_op jit(solution)/shard_map/while/body/eval_jaxpr/while/body/tkgd,nkd->tkgn/dot_general | solution.py:74
  63.2 3.7 %bitcast_add_fusion.5 = f32[512,1,8,128]{0,3,2,1:T(8,128)S(1)} fusion(f32[512,1,8,128]{0,3,2,1:T(8,128)S(1)} %get-tuple-element.279, f32[512,512,8]{1,0,2:T(8,128)S(1)} %get-tuple-element.260, f32[512,8]{0,1:T(8,128)S(1)} %bitcast.106, pred[512,512]{0,1:T(8,128)(4,1)S(1)} %compare_and_fusion.2, f32[512,8]{0,1:T(8,128)S(1)} %get-tuple-element.261, ...), kind=kOutput, calls=%fused_computation.9.clone.1 | convolution fusion | flops 548405248 | bytes 13008900 | tf_op jit(solution)/shard_map/while/body/eval_jaxpr/while/body/tkgn,nkd->tkgd/dot_general | solution.py:84
  67.0 2.0 %fusion.33 = f32[512,8]{0,1:T(8,128)S(1)} fusion(f32[512,512,8]{1,0,2:T(8,128)S(1)} %get-tuple-element.260, f32[512,8]{0,1:T(8,128)S(1)} %bitcast.107, pred[512,512]{0,1:T(8,128)(4,1)S(1)} %compare_and_fusion.2), kind=kLoop, calls=%fused_computation.5.clone.1 | loop fusion | flops 10481664 | bytes 8683520 | tf_op jit(solution)/shard_map/while/body/eval_jaxpr/while/body/reduce_sum | solution.py:83
  69.7 1.0 %divide_convert_fusion = bf16[512,1,8,128]{0,3,2,1:T(8,128)(2,1)S(1)} fusion(f32[512,1,8,128]{0,3,2,1:T(8,128)S(1)} %get-tuple-element.108, f32[512,8]{0,1:T(8,128)} %bitcast.112), kind=kLoop, calls=%fused_computation.28 | loop fusion | flops 1048576 | bytes 3162112 | tf_op jit(solution)/shard_map/while/body/eval_jaxpr/convert_element_type | solution.py:103
  71.6 17.1 %all_to_all.73 = bf16[4,128,1024]{2,1,0:T(8,128)(2,1)S(1)} all-to-all(bf16[4,128,1024]{2,1,0:T(8,128)(2,1)S(1)} %copy.32), channel_id=1, replica_groups=mesh['blk'=8,'uly'=4] {'uly'}, dimensions={0} | all-to-all | bytes 2097152 | tf_op jit(solution)/shard_map/all_to_all | solution.py:107
  89.4 1.3 %copy.30 = bf16[128,4096]{1,0:T(8,128)(2,1)} copy(bf16[128,4096]{0,1:T(8,128)(2,1)S(1)} %bitcast.110) | data formatting | bytes 2097152 | tf_op jit(solution)/shard_map/all_to_all | solution.py:107
  (39 shorter events, 5.6 us)
Async XLA Ops:
  0.0 5.0 %copy-start = (bf16[128,512]{1,0:T(8,128)(2,1)S(1)}, bf16[128,512]{1,0:T(8,128)(2,1)}, u32[]{:S(2)}) copy-start(bf16[128,512]{1,0:T(8,128)(2,1)} %param.7) | copy-start | bytes 393220
  1.7 7.9 %all-to-all-start.2 = ((bf16[128,4,128]{0,2,1:T(8,128)(2,1)}), bf16[128,4,128]{0,2,1:T(8,128)(2,1)S(1)}, u32[]{:S(2)}, u32[]{:S(2)}) async-start(bf16[128,4,128]{0,2,1:T(8,128)(2,1)} %bitcast.5), calls=%async_computation.2 | async-start | bytes 262144 | tf_op jit(solution)/shard_map/all_to_all | solution.py:32
  9.6 7.9 %all-to-all-start = ((bf16[128,4,128]{2,0,1:T(8,128)(2,1)}), bf16[128,4,128]{2,0,1:T(8,128)(2,1)S(1)}, u32[]{:S(2)}, u32[]{:S(2)}) async-start(bf16[128,4,128]{2,0,1:T(8,128)(2,1)} %copy_bitcast_fusion.1), calls=%async_computation | async-start | bytes 262144 | tf_op jit(solution)/shard_map/all_to_all | solution.py:31
  17.5 21.4 %all-to-all-start.1 = ((bf16[128,4,1024]{2,0,1:T(8,128)(2,1)}), bf16[128,4,1024]{2,0,1:T(8,128)(2,1)S(1)}, u32[]{:S(2)}, u32[]{:S(2)}) async-start(bf16[128,4,1024]{2,0,1:T(8,128)(2,1)} %bitcast.83), calls=%async_computation.1 | async-start | bytes 2097152 | tf_op jit(solution)/shard_map/all_to_all | solution.py:29
  21.2 11.6 %collective-permute-start.2 = (bf16[512,128]{1,0:T(8,128)(2,1)S(1)}, bf16[512,128]{1,0:T(8,128)(2,1)S(1)}, u32[]{:S(2)}, u32[]{:S(2)}) collective-permute-start(bf16[512,128]{1,0:T(8,128)(2,1)S(1)} %bitcast.116), channel_id=1, source_target_pairs={{0,8},{4,12},{8,16},{12,20},{16,24},{20,28},{1,9},{5,13},{9,17},{1... | collective-permute-start | bytes 393224 | tf_op jit(solution)/shard_map/ppermute | solution.py:15
  24.7 8.1 %collective-permute-start.3 = (bf16[512,128]{1,0:T(8,128)(2,1)S(1)}, bf16[512,128]{1,0:T(8,128)(2,1)S(1)}, u32[]{:S(2)}, u32[]{:S(2)}) collective-permute-start(bf16[512,128]{1,0:T(8,128)(2,1)S(1)} %bitcast.117), channel_id=1, source_target_pairs={{0,4},{4,8},{8,12},{12,16},{16,20},{20,24},{24,28},{1,5},{5,9},{9,... | collective-permute-start | bytes 393224 | tf_op jit(solution)/shard_map/ppermute | solution.py:15
  28.7 7.5 %collective-permute-start = (bf16[512,128]{1,0:T(8,128)(2,1)S(1)}, bf16[512,128]{1,0:T(8,128)(2,1)S(1)}, u32[]{:S(2)}, u32[]{:S(2)}) collective-permute-start(bf16[512,128]{1,0:T(8,128)(2,1)S(1)} %bitcast.113), channel_id=1, source_target_pairs={{0,8},{4,12},{8,16},{12,20},{16,24},{20,28},{1,9},{5,13},{9,17},{1... | collective-permute-start | bytes 393224 | tf_op jit(solution)/shard_map/ppermute | solution.py:15
  30.6 7.5 %collective-permute-start.1 = (bf16[512,128]{1,0:T(8,128)(2,1)S(1)}, bf16[512,128]{1,0:T(8,128)(2,1)S(1)}, u32[]{:S(2)}, u32[]{:S(2)}) collective-permute-start(bf16[512,128]{1,0:T(8,128)(2,1)S(1)} %bitcast.114), channel_id=1, source_target_pairs={{0,4},{4,8},{8,12},{12,16},{16,20},{20,24},{24,28},{1,5},{5,9},{9,... | collective-permute-start | bytes 393224 | tf_op jit(solution)/shard_map/ppermute | solution.py:15
  43.6 5.8 %copy-start.1 = (f32[512,1,8]{0,2,1:T(8,128)S(1)}, f32[512,1,8]{0,2,1:T(8,128)}, u32[]{:S(2)}) copy-start(f32[512,1,8]{0,2,1:T(8,128)} %get-tuple-element.278) | copy-start | bytes 49156 | tf_op jit(solution)/shard_map/while/body/eval_jaxpr/while
  49.4 0.6 copy-start.2
  53.4 5.8 %copy-start.1 = (f32[512,1,8]{0,2,1:T(8,128)S(1)}, f32[512,1,8]{0,2,1:T(8,128)}, u32[]{:S(2)}) copy-start(f32[512,1,8]{0,2,1:T(8,128)} %get-tuple-element.278) | copy-start | bytes 49156 | tf_op jit(solution)/shard_map/while/body/eval_jaxpr/while
  59.2 0.6 copy-start.2
  63.2 5.8 %copy-start.1 = (f32[512,1,8]{0,2,1:T(8,128)S(1)}, f32[512,1,8]{0,2,1:T(8,128)}, u32[]{:S(2)}) copy-start(f32[512,1,8]{0,2,1:T(8,128)} %get-tuple-element.278) | copy-start | bytes 49156 | tf_op jit(solution)/shard_map/while/body/eval_jaxpr/while
  69.0 0.6 copy-start.2
where the time goes:
time: 91.6 us; the launch traced here: 90.7 us
  starting transfers between devices  19.6 us (21%)
  matrix products  18.4 us (20%)
  blocking collectives  17.1 us (19%)
  other arithmetic  13 us (14%)
  local copies, waits for them, and re-layouts  10.8 us (12%)
  waiting for transfers between devices  10.7 us (12%)
    all_to_all x1, blocking collectives, local(): return lax.all_to_all(attn, 'uly', split_axis=0, concat_axis=1, tiled=True)  17.1 us
    dot_general x3, matrix products, add_tile(): jnp.einsum('tkgn,nkd->tkgd', exps.astype(jnp.bfloat16), value_tile, prefe...  11.2 us
    ppermute x4, starting transfers between devices, from_behind(): return lax.ppermute(block, axis, route)  9.44 us
    dot_general x3, matrix products, add_tile(): jnp.einsum('tkgd,nkd->tkgn', query_tile, key_tile, preferred_element_type...  7.21 us
    reduce_sum x3, other arithmetic, add_tile(): running_sum = running_sum * factor + jnp.sum(exps, axis=-1)  6.1 us
    ppermute x4, waiting for transfers between devices, from_behind(): return lax.ppermute(block, axis, route)  4.56 us
    all_to_all x1, waiting for transfers between devices, local(): lax.all_to_all(widen_heads(value_projection), 'uly', split_axis=1, concat...  3.88 us
    all_to_all x1, starting transfers between devices, local(): lax.all_to_all(query_projection, 'uly', split_axis=1, concat_axis=0, tile...  3.52 us
  transfers between devices with their start and end apart: 7, of which 4 were waited for; matrix products, arithmetic and copies ran while one was open for 7% of the time, Pallas kernels for 0%

commit v1 on v0

--- a/solution.py
+++ b/solution.py
@@ -2,11 +2,33 @@
 import jax.numpy as jnp
 from jax import lax
 from jax.sharding import PartitionSpec as P
+from jax.lax import axis_index, axis_size, ppermute
 
 HEAD_WIDTH = 128
 CYCLE_STEPS = 2
 POSITION_GROUP = 512
 masked_score = -1e30
+
+
+def read_the_sides(x_local, d_out, local_values):
+    small = x_local.shape
+    return jnp.moveaxis(
+        x_local.reshape(
+            *small[:d_out], local_values, small[d_out] // local_values, *small[d_out + 1 :]
+        ),
+        d_out,
+        0,
+    )
+
+
+def launch_ladders(v0, along_dim):
+    v0 = jnp.moveaxis(v0, 0, along_dim)
+    mixed_arr = v0.shape
+    return v0.reshape(
+        *mixed_arr[:along_dim],
+        mixed_arr[along_dim] * mixed_arr[along_dim + 1],
+        *mixed_arr[along_dim + 2 :]
+    )
 
 
 def from_behind(block, axis, distance):
@@ -26,7 +48,17 @@
         copies = jnp.broadcast_to(split_heads, (tokens_dev, kv_heads, repeats, HEAD_WIDTH))
         return copies.reshape(tokens_dev, kv_heads * repeats * HEAD_WIDTH)
 
-    query_rows = lax.all_to_all(query_projection, "uly", split_axis=1, concat_axis=0, tiled=True)
+    current_block = axis_size("uly")
+    low = axis_index("uly")
+    v1, plain = (current_block, low)
+    h_now = read_the_sides(query_projection, 1, v1)
+    found = [h_now[plain]]
+    for w in range(1, v1):
+        b_now = h_now[plain ^ w]
+        y2 = ppermute(b_now, "uly", [(pp, pp ^ w) for pp in range(v1)])
+        found.append(y2)
+    h_now = jnp.stack(found, axis=0)[plain ^ jnp.arange(v1)]
+    query_rows = launch_ladders(h_now, 0)
     key_rows, value_rows = (
         lax.all_to_all(widen_heads(key_projection), "uly", split_axis=1, concat_axis=0, tiled=True),
         lax.all_to_all(

time: 91.6 us -> 94.2 us (1.028)
  starting transfers between devices: 19.6 us -> 21.6 us
    all_to_all x1 -> x0, starting transfers between devices: 3.52 us -> none  [local(): lax.all_to_all(query_projection, 'uly', split_axis=1, concat_axis=0, tile...]
    all_to_all x1, waiting for transfers between devices: 3.88 us -> 7.38 us  [local(): lax.all_to_all(widen_heads(value_projection), 'uly', split_axis=1, concat...]
    ppermute x4, starting transfers between devices: 9.44 us -> 12.6 us  [from_behind(): return lax.ppermute(block, axis, route)]
    ppermute x0 -> x3, starting transfers between devices: none -> 2.34 us  [local(): y2 = ppermute(b_now, 'uly', [(pp, pp ^ w) for pp in range(v1)])]
    all_to_all x1 -> x0, local copies, waits for them, and re-layouts: 2.29 us -> none  [local(): lax.all_to_all(query_projection, 'uly', split_axis=1, concat_axis=0, tile...]
    all_to_all x1, waiting for transfers between devices: 2.28 us -> 0.01 us  [local(): lax.all_to_all(widen_heads(key_projection), 'uly', split_axis=1, concat_a...]
    unnamed x5 -> x6, local copies, waits for them, and re-layouts: 2.11 us -> 3.71 us
    ppermute x4, waiting for transfers between devices: 4.56 us -> 3.02 us  [from_behind(): return lax.ppermute(block, axis, route)]
  transfers between devices with their start and end apart: 7 -> 9, of which waited for: 4 -> 3; matrix products, arithmetic and copies ran while one was open for 7% -> 6% of each run, Pallas kernels for 0% -> 0%
where the time goes in v1:
time: 94.2 us; the launch traced here: 93.4 us
  starting transfers between devices  21.6 us (23%)
  matrix products  18.4 us (20%)
  blocking collectives  17.5 us (19%)
  other arithmetic  13.1 us (14%)
  local copies, waits for them, and re-layouts  11.4 us (12%)
  waiting for transfers between devices  10.4 us (11%)
    all_to_all x1, blocking collectives, local(): return lax.all_to_all(attn, 'uly', split_axis=0, concat_axis=1, tiled=True)  17.5 us
    ppermute x4, starting transfers between devices, from_behind(): return lax.ppermute(block, axis, route)  12.6 us
    dot_general x3, matrix products, add_tile(): jnp.einsum('tkgn,nkd->tkgd', exps.astype(jnp.bfloat16), value_tile, prefe...  11.2 us
    all_to_all x1, waiting for transfers between devices, local(): lax.all_to_all(widen_heads(value_projection), 'uly', split_axis=1, concat...  7.38 us
    dot_general x3, matrix products, add_tile(): jnp.einsum('tkgd,nkd->tkgn', query_tile, key_tile, preferred_element_type...  7.21 us
    reduce_sum x3, other arithmetic, add_tile(): running_sum = running_sum * factor + jnp.sum(exps, axis=-1)  6.1 us
    unnamed x6, local copies, waits for them, and re-layouts  3.71 us
    all_to_all x1, starting transfers between devices, local(): lax.all_to_all(widen_heads(key_projection), 'uly', split_axis=1, concat_a...  3.33 us
  transfers between devices with their start and end apart: 9, of which 3 were waited for; matrix products, arithmetic and copies ran while one was open for 6% of the time, Pallas kernels for 0%

profile of v1, /device:TPU:18, one launch (start us, length us, event | category | flops | bytes accessed | tf_op | source)
XLA Modules:
  0.0 93.4 jit_solution(2708339761849453535)
XLA Ops:
  0.0 1.6 %copy.36 = bf16[128,4096]{0,1:T(8,128)(2,1)S(1)} copy(bf16[128,4096]{1,0:T(8,128)(2,1)} %param.6) | data formatting | bytes 2097152 | tf_op args[0]
  1.9 1.0 %collective-permute-start.4 = (bf16[128,1024]{1,0:T(8,128)(2,1)S(1)}, bf16[128,1024]{1,0:T(8,128)(2,1)S(1)}, u32[]{:S(2)}, u32[]{:S(2)}) collective-permute-start(bf16[128,1024]{1,0:T(8,128)(2,1)S(1)} %bitcast.125), channel_id=1, source_target_pairs={{0,3},{1,2},{2,1},{3,0},{4,7},{5,6},{6,5},{7,4},{8,11},{9,10},{10,... | collective-permute-start | bytes 786440 | tf_op jit(solution)/shard_map/ppermute | solution.py:58
  3.1 0.7 collective-permute-start.2
  4.6 1.7 %copy.41 = bf16[128,512]{0,1:T(8,128)(2,1)} copy(bf16[128,512]{1,0:T(8,128)(2,1)} %param.8) | data formatting | bytes 262144 | tf_op args[2]
  6.2 3.3 %all-to-all-start.1 = ((bf16[128,4,128]{0,2,1:T(8,128)(2,1)}), bf16[128,4,128]{0,2,1:T(8,128)(2,1)S(1)}, u32[]{:S(2)}, u32[]{:S(2)}) async-start(bf16[128,4,128]{0,2,1:T(8,128)(2,1)} %bitcast.13), calls=%async_computation.1 | async-start | bytes 262144 | tf_op jit(solution)/shard_map/all_to_all | solution.py:64
  9.5 0.7 copy_bitcast_fusion
  10.2 7.4 %all-to-all-done.1 = bf16[128,4,128]{0,2,1:T(8,128)(2,1)S(1)} async-done(((bf16[128,4,128]{0,2,1:T(8,128)(2,1)}), bf16[128,4,128]{0,2,1:T(8,128)(2,1)S(1)}, u32[]{:S(2)}, u32[]{:S(2)}) %all-to-all-start.1) | async-done | bytes 131104 | tf_op jit(solution)/shard_map/all_to_all | solution.py:64
  17.6 3.3 %all-to-all-start = ((bf16[128,4,128]{2,0,1:T(8,128)(2,1)}), bf16[128,4,128]{2,0,1:T(8,128)(2,1)S(1)}, u32[]{:S(2)}, u32[]{:S(2)}) async-start(bf16[128,4,128]{2,0,1:T(8,128)(2,1)} %copy_bitcast_fusion), calls=%async_computation | async-start | bytes 262144 | tf_op jit(solution)/shard_map/all_to_all | solution.py:63
  21.1 3.5 %collective-permute-start.5 = (bf16[512,128]{1,0:T(8,128)(2,1)S(1)}, bf16[512,128]{1,0:T(8,128)(2,1)S(1)}, u32[]{:S(2)}, u32[]{:S(2)}) collective-permute-start(bf16[512,128]{1,0:T(8,128)(2,1)S(1)} %bitcast.122), channel_id=1, source_target_pairs={{0,8},{4,12},{8,16},{12,20},{16,24},{20,28},{1,9},{5,13},{9,17},{1... | collective-permute-start | bytes 393224 | tf_op jit(solution)/shard_map/ppermute | solution.py:37
  24.6 1.9 %collective-permute-start.6 = (bf16[512,128]{1,0:T(8,128)(2,1)S(1)}, bf16[512,128]{1,0:T(8,128)(2,1)S(1)}, u32[]{:S(2)}, u32[]{:S(2)}) collective-permute-start(bf16[512,128]{1,0:T(8,128)(2,1)S(1)} %bitcast.123), channel_id=1, source_target_pairs={{0,4},{4,8},{8,12},{12,16},{16,20},{20,24},{24,28},{1,5},{5,9},{9,... | collective-permute-start | bytes 393224 | tf_op jit(solution)/shard_map/ppermute | solution.py:37
  26.5 1.3 %reduce_min.10 = s32[]{:T(128)} reduce(s32[512]{0:T(512)} %param.9, s32[]{:T(128)} %constant.101.clone.1), dimensions={0}, to_apply=%region_0.1 | reduce | flops 511 | bytes 2056 | tf_op jit(solution)/shard_map/while/body/eval_jaxpr/reduce_min | solution.py:92
  28.8 4.0 %collective-permute-start = (bf16[512,128]{1,0:T(8,128)(2,1)S(1)}, bf16[512,128]{1,0:T(8,128)(2,1)S(1)}, u32[]{:S(2)}, u32[]{:S(2)}) collective-permute-start(bf16[512,128]{1,0:T(8,128)(2,1)S(1)} %bitcast.119), channel_id=1, source_target_pairs={{0,8},{4,12},{8,16},{12,20},{16,24},{20,28},{1,9},{5,13},{9,17},{1... | collective-permute-start | bytes 393224 | tf_op jit(solution)/shard_map/ppermute | solution.py:37
  32.8 3.2 %collective-permute-start.1 = (bf16[512,128]{1,0:T(8,128)(2,1)S(1)}, bf16[512,128]{1,0:T(8,128)(2,1)S(1)}, u32[]{:S(2)}, u32[]{:S(2)}) collective-permute-start(bf16[512,128]{1,0:T(8,128)(2,1)S(1)} %bitcast.120), channel_id=1, source_target_pairs={{0,4},{4,8},{8,12},{12,16},{16,20},{20,24},{24,28},{1,5},{5,9},{9,... | collective-permute-start | bytes 393224 | tf_op jit(solution)/shard_map/ppermute | solution.py:37
  36.0 0.8 maximum_bitcast_fusion.1
  36.8 2.9 %collective-permute-done.1 = bf16[512,128]{1,0:T(8,128)(2,1)S(1)} collective-permute-done((bf16[512,128]{1,0:T(8,128)(2,1)S(1)}, bf16[512,128]{1,0:T(8,128)(2,1)S(1)}, u32[]{:S(2)}, u32[]{:S(2)}) %collective-permute-start.1) | collective-permute-done | bytes 131104 | tf_op jit(solution)/shard_map/ppermute | solution.py:37
  39.7 0.8 maximum_bitcast_fusion
  42.5 29.5 %while.24 = (s32[]{:T(128)}, f32[512,1,8]{0,2,1:T(8,128)S(1)}, f32[512,1,8]{0,2,1:T(8,128)}, f32[512,1,8,128]{0,3,2,1:T(8,128)S(1)}, s32[]{:T(128)}, /*index=5*/...) while((s32[]{:T(128)}, f32[512,1,8]{0,2,1:T(8,128)S(1)}, ...), condition=%wide.region_4.5_spmd.clone, body=%wide.region_1.4_spmd.clone.sunk | while | flops 1102853120 | bytes 32123144 | solution.py:132
  42.5 0.9 %compare_and_fusion.2 = pred[512,512]{0,1:T(8,128)(4,1)S(1)} fusion(s32[512]{0:T(512)S(1)} %get-tuple-element.270, s32[512]{0:T(512)} %get-tuple-element.309, s32[512]{0:T(512)S(1)} %get-tuple-element.271), kind=kLoop, calls=%fused_computation.13.clone.1 | loop fusion | flops 786432 | bytes 268288 | tf_op jit(solution)/shard_map/while/body/eval_jaxpr/while/body/and | solution.py:101
  43.5 2.4 %fusion.32 = (f32[512,8]{0,1:T(8,128)S(1)}, f32[512,512,8]{1,0,2:T(8,128)S(1)}) fusion(pred[512,512]{0,1:T(8,128)(4,1)S(1)} %compare_and_fusion.2, bf16[512,1,8,128]{3,0,2,1:T(8,128)(2,1)S(1)} %get-tuple-element.311, bf16[1536,1,128]{2,0,1:T(8,128)(2,1)} %get-tuple-element.310, s32[]{:T(128)S(6)} %select_n.94), kind=kOutput, calls=%fused_computation.4.clone.1 | convolution fusion | flops 543158272 | bytes 9846788 | tf_op jit(solution)/shard_map/while/body/eval_jaxpr/while/body/tkgd,nkd->tkgn/dot_general | solution.py:106
  45.9 3.7 %bitcast_add_fusion.5 = f32[512,1,8,128]{0,3,2,1:T(8,128)S(1)} fusion(f32[512,1,8,128]{0,3,2,1:T(8,128)S(1)} %get-tuple-element.293, f32[512,512,8]{1,0,2:T(8,128)S(1)} %get-tuple-element.274, f32[512,8]{0,1:T(8,128)S(1)} %bitcast.111, pred[512,512]{0,1:T(8,128)(4,1)S(1)} %compare_and_fusion.2, f32[512,8]{0,1:T(8,128)S(1)} %get-tuple-element.275, ...), kind=kOutput, calls=%fused_computation.10.clone.1 | convolution fusion | flops 548405248 | bytes 13008900 | tf_op jit(solution)/shard_map/while/body/eval_jaxpr/while/body/tkgn,nkd->tkgd/dot_general | solution.py:116
  49.7 2.0 %fusion.34 = f32[512,8]{0,1:T(8,128)S(1)} fusion(f32[512,512,8]{1,0,2:T(8,128)S(1)} %get-tuple-element.274, f32[512,8]{0,1:T(8,128)S(1)} %bitcast.112, pred[512,512]{0,1:T(8,128)(4,1)S(1)} %compare_and_fusion.2), kind=kLoop, calls=%fused_computation.6.clone.1 | loop fusion | flops 10481664 | bytes 8683520 | tf_op jit(solution)/shard_map/while/body/eval_jaxpr/while/body/reduce_sum | solution.py:115
  52.4 0.9 %compare_and_fusion.2 = pred[512,512]{0,1:T(8,128)(4,1)S(1)} fusion(s32[512]{0:T(512)S(1)} %get-tuple-element.270, s32[512]{0:T(512)} %get-tuple-element.309, s32[512]{0:T(512)S(1)} %get-tuple-element.271), kind=kLoop, calls=%fused_computation.13.clone.1 | loop fusion | flops 786432 | bytes 268288 | tf_op jit(solution)/shard_map/while/body/eval_jaxpr/while/body/and | solution.py:101
  53.3 2.4 %fusion.32 = (f32[512,8]{0,1:T(8,128)S(1)}, f32[512,512,8]{1,0,2:T(8,128)S(1)}) fusion(pred[512,512]{0,1:T(8,128)(4,1)S(1)} %compare_and_fusion.2, bf16[512,1,8,128]{3,0,2,1:T(8,128)(2,1)S(1)} %get-tuple-element.311, bf16[1536,1,128]{2,0,1:T(8,128)(2,1)} %get-tuple-element.310, s32[]{:T(128)S(6)} %select_n.94), kind=kOutput, calls=%fused_computation.4.clone.1 | convolution fusion | flops 543158272 | bytes 9846788 | tf_op jit(solution)/shard_map/while/body/eval_jaxpr/while/body/tkgd,nkd->tkgn/dot_general | solution.py:106
  55.8 3.7 %bitcast_add_fusion.5 = f32[512,1,8,128]{0,3,2,1:T(8,128)S(1)} fusion(f32[512,1,8,128]{0,3,2,1:T(8,128)S(1)} %get-tuple-element.293, f32[512,512,8]{1,0,2:T(8,128)S(1)} %get-tuple-element.274, f32[512,8]{0,1:T(8,128)S(1)} %bitcast.111, pred[512,512]{0,1:T(8,128)(4,1)S(1)} %compare_and_fusion.2, f32[512,8]{0,1:T(8,128)S(1)} %get-tuple-element.275, ...), kind=kOutput, calls=%fused_computation.10.clone.1 | convolution fusion | flops 548405248 | bytes 13008900 | tf_op jit(solution)/shard_map/while/body/eval_jaxpr/while/body/tkgn,nkd->tkgd/dot_general | solution.py:116
  59.5 2.0 %fusion.34 = f32[512,8]{0,1:T(8,128)S(1)} fusion(f32[512,512,8]{1,0,2:T(8,128)S(1)} %get-tuple-element.274, f32[512,8]{0,1:T(8,128)S(1)} %bitcast.112, pred[512,512]{0,1:T(8,128)(4,1)S(1)} %compare_and_fusion.2), kind=kLoop, calls=%fused_computation.6.clone.1 | loop fusion | flops 10481664 | bytes 8683520 | tf_op jit(solution)/shard_map/while/body/eval_jaxpr/while/body/reduce_sum | solution.py:115
  62.2 0.9 %compare_and_fusion.2 = pred[512,512]{0,1:T(8,128)(4,1)S(1)} fusion(s32[512]{0:T(512)S(1)} %get-tuple-element.270, s32[512]{0:T(512)} %get-tuple-element.309, s32[512]{0:T(512)S(1)} %get-tuple-element.271), kind=kLoop, calls=%fused_computation.13.clone.1 | loop fusion | flops 786432 | bytes 268288 | tf_op jit(solution)/shard_map/while/body/eval_jaxpr/while/body/and | solution.py:101
  63.1 2.4 %fusion.32 = (f32[512,8]{0,1:T(8,128)S(1)}, f32[512,512,8]{1,0,2:T(8,128)S(1)}) fusion(pred[512,512]{0,1:T(8,128)(4,1)S(1)} %compare_and_fusion.2, bf16[512,1,8,128]{3,0,2,1:T(8,128)(2,1)S(1)} %get-tuple-element.311, bf16[1536,1,128]{2,0,1:T(8,128)(2,1)} %get-tuple-element.310, s32[]{:T(128)S(6)} %select_n.94), kind=kOutput, calls=%fused_computation.4.clone.1 | convolution fusion | flops 543158272 | bytes 9846788 | tf_op jit(solution)/shard_map/while/body/eval_jaxpr/while/body/tkgd,nkd->tkgn/dot_general | solution.py:106
  65.6 3.7 %bitcast_add_fusion.5 = f32[512,1,8,128]{0,3,2,1:T(8,128)S(1)} fusion(f32[512,1,8,128]{0,3,2,1:T(8,128)S(1)} %get-tuple-element.293, f32[512,512,8]{1,0,2:T(8,128)S(1)} %get-tuple-element.274, f32[512,8]{0,1:T(8,128)S(1)} %bitcast.111, pred[512,512]{0,1:T(8,128)(4,1)S(1)} %compare_and_fusion.2, f32[512,8]{0,1:T(8,128)S(1)} %get-tuple-element.275, ...), kind=kOutput, calls=%fused_computation.10.clone.1 | convolution fusion | flops 548405248 | bytes 13008900 | tf_op jit(solution)/shard_map/while/body/eval_jaxpr/while/body/tkgn,nkd->tkgd/dot_general | solution.py:116
  69.3 2.0 %fusion.34 = f32[512,8]{0,1:T(8,128)S(1)} fusion(f32[512,512,8]{1,0,2:T(8,128)S(1)} %get-tuple-element.274, f32[512,8]{0,1:T(8,128)S(1)} %bitcast.112, pred[512,512]{0,1:T(8,128)(4,1)S(1)} %compare_and_fusion.2), kind=kLoop, calls=%fused_computation.6.clone.1 | loop fusion | flops 10481664 | bytes 8683520 | tf_op jit(solution)/shard_map/while/body/eval_jaxpr/while/body/reduce_sum | solution.py:115
  72.0 1.0 %divide_convert_fusion = bf16[512,1,8,128]{0,3,2,1:T(8,128)(2,1)S(1)} fusion(f32[512,1,8,128]{0,3,2,1:T(8,128)S(1)} %get-tuple-element.108, f32[512,8]{0,1:T(8,128)} %bitcast.118), kind=kLoop, calls=%fused_computation.29 | loop fusion | flops 1048576 | bytes 3162112 | tf_op jit(solution)/shard_map/while/body/eval_jaxpr/convert_element_type | solution.py:135
  74.0 17.5 %all_to_all.57 = bf16[4,128,1024]{2,1,0:T(8,128)(2,1)S(1)} all-to-all(bf16[4,128,1024]{2,1,0:T(8,128)(2,1)S(1)} %copy.49), channel_id=1, replica_groups=mesh['blk'=8,'uly'=4] {'uly'}, dimensions={0} | all-to-all | bytes 2097152 | tf_op jit(solution)/shard_map/all_to_all | solution.py:139
  92.1 1.3 %copy.47 = bf16[128,4096]{1,0:T(8,128)(2,1)} copy(bf16[128,4096]{0,1:T(8,128)(2,1)S(1)} %bitcast.116) | data formatting | bytes 2097152 | tf_op jit(solution)/shard_map/all_to_all | solution.py:139
  (52 shorter events, 7.0 us)
Async XLA Ops:
  0.0 9.5 %copy-start = (bf16[128,512]{1,0:T(8,128)(2,1)S(1)}, bf16[128,512]{1,0:T(8,128)(2,1)}, u32[]{:S(2)}) copy-start(bf16[128,512]{1,0:T(8,128)(2,1)} %param.7) | copy-start | bytes 393220
  1.9 38.6 %collective-permute-start.4 = (bf16[128,1024]{1,0:T(8,128)(2,1)S(1)}, bf16[128,1024]{1,0:T(8,128)(2,1)S(1)}, u32[]{:S(2)}, u32[]{:S(2)}) collective-permute-start(bf16[128,1024]{1,0:T(8,128)(2,1)S(1)} %bitcast.125), channel_id=1, source_target_pairs={{0,3},{1,2},{2,1},{3,0},{4,7},{5,6},{6,5},{7,4},{8,11},{9,10},{10,... | collective-permute-start | bytes 786440 | tf_op jit(solution)/shard_map/ppermute | solution.py:58
  3.1 37.4 %collective-permute-start.2 = (bf16[128,1024]{1,0:T(8,128)(2,1)S(1)}, bf16[128,1024]{1,0:T(8,128)(2,1)S(1)}, u32[]{:S(2)}, u32[]{:S(2)}) collective-permute-start(bf16[128,1024]{1,0:T(8,128)(2,1)S(1)} %bitcast.126), channel_id=1, source_target_pairs={{0,1},{1,0},{2,3},{3,2},{4,5},{5,4},{6,7},{7,6},{8,9},{9,8},{10,11... | collective-permute-start | bytes 786440 | tf_op jit(solution)/shard_map/ppermute | solution.py:58
  4.0 36.5 %collective-permute-start.3 = (bf16[128,1024]{1,0:T(8,128)(2,1)S(1)}, bf16[128,1024]{1,0:T(8,128)(2,1)S(1)}, u32[]{:S(2)}, u32[]{:S(2)}) collective-permute-start(bf16[128,1024]{1,0:T(8,128)(2,1)S(1)} %bitcast.127), channel_id=1, source_target_pairs={{0,2},{1,3},{2,0},{3,1},{4,6},{5,7},{6,4},{7,5},{8,10},{9,11},{10,... | collective-permute-start | bytes 786440 | tf_op jit(solution)/shard_map/ppermute | solution.py:58
  6.2 11.4 %all-to-all-start.1 = ((bf16[128,4,128]{0,2,1:T(8,128)(2,1)}), bf16[128,4,128]{0,2,1:T(8,128)(2,1)S(1)}, u32[]{:S(2)}, u32[]{:S(2)}) async-start(bf16[128,4,128]{0,2,1:T(8,128)(2,1)} %bitcast.13), calls=%async_computation.1 | async-start | bytes 262144 | tf_op jit(solution)/shard_map/all_to_all | solution.py:64
  17.6 11.1 %all-to-all-start = ((bf16[128,4,128]{2,0,1:T(8,128)(2,1)}), bf16[128,4,128]{2,0,1:T(8,128)(2,1)S(1)}, u32[]{:S(2)}, u32[]{:S(2)}) async-start(bf16[128,4,128]{2,0,1:T(8,128)(2,1)} %copy_bitcast_fusion), calls=%async_computation | async-start | bytes 262144 | tf_op jit(solution)/shard_map/all_to_all | solution.py:63
  21.1 7.8 %collective-permute-start.5 = (bf16[512,128]{1,0:T(8,128)(2,1)S(1)}, bf16[512,128]{1,0:T(8,128)(2,1)S(1)}, u32[]{:S(2)}, u32[]{:S(2)}) collective-permute-start(bf16[512,128]{1,0:T(8,128)(2,1)S(1)} %bitcast.122), channel_id=1, source_target_pairs={{0,8},{4,12},{8,16},{12,20},{16,24},{20,28},{1,9},{5,13},{9,17},{1... | collective-permute-start | bytes 393224 | tf_op jit(solution)/shard_map/ppermute | solution.py:37
  24.6 8.3 %collective-permute-start.6 = (bf16[512,128]{1,0:T(8,128)(2,1)S(1)}, bf16[512,128]{1,0:T(8,128)(2,1)S(1)}, u32[]{:S(2)}, u32[]{:S(2)}) collective-permute-start(bf16[512,128]{1,0:T(8,128)(2,1)S(1)} %bitcast.123), channel_id=1, source_target_pairs={{0,4},{4,8},{8,12},{12,16},{16,20},{20,24},{24,28},{1,5},{5,9},{9,... | collective-permute-start | bytes 393224 | tf_op jit(solution)/shard_map/ppermute | solution.py:37
  28.8 8.0 %collective-permute-start = (bf16[512,128]{1,0:T(8,128)(2,1)S(1)}, bf16[512,128]{1,0:T(8,128)(2,1)S(1)}, u32[]{:S(2)}, u32[]{:S(2)}) collective-permute-start(bf16[512,128]{1,0:T(8,128)(2,1)S(1)} %bitcast.119), channel_id=1, source_target_pairs={{0,8},{4,12},{8,16},{12,20},{16,24},{20,28},{1,9},{5,13},{9,17},{1... | collective-permute-start | bytes 393224 | tf_op jit(solution)/shard_map/ppermute | solution.py:37
  32.8 6.9 %collective-permute-start.1 = (bf16[512,128]{1,0:T(8,128)(2,1)S(1)}, bf16[512,128]{1,0:T(8,128)(2,1)S(1)}, u32[]{:S(2)}, u32[]{:S(2)}) collective-permute-start(bf16[512,128]{1,0:T(8,128)(2,1)S(1)} %bitcast.120), channel_id=1, source_target_pairs={{0,4},{4,8},{8,12},{12,16},{16,20},{20,24},{24,28},{1,5},{5,9},{9,... | collective-permute-start | bytes 393224 | tf_op jit(solution)/shard_map/ppermute | solution.py:37
  45.9 5.8 %copy-start.1 = (f32[512,1,8]{0,2,1:T(8,128)S(1)}, f32[512,1,8]{0,2,1:T(8,128)}, u32[]{:S(2)}) copy-start(f32[512,1,8]{0,2,1:T(8,128)} %get-tuple-element.292) | copy-start | bytes 49156 | tf_op jit(solution)/shard_map/while/body/eval_jaxpr/while
  51.8 0.6 copy-start.2
  55.8 5.8 %copy-start.1 = (f32[512,1,8]{0,2,1:T(8,128)S(1)}, f32[512,1,8]{0,2,1:T(8,128)}, u32[]{:S(2)}) copy-start(f32[512,1,8]{0,2,1:T(8,128)} %get-tuple-element.292) | copy-start | bytes 49156 | tf_op jit(solution)/shard_map/while/body/eval_jaxpr/while
  61.6 0.6 copy-start.2
  65.6 5.8 %copy-start.1 = (f32[512,1,8]{0,2,1:T(8,128)S(1)}, f32[512,1,8]{0,2,1:T(8,128)}, u32[]{:S(2)}) copy-start(f32[512,1,8]{0,2,1:T(8,128)} %get-tuple-element.292) | copy-start | bytes 49156 | tf_op jit(solution)/shard_map/while/body/eval_jaxpr/while
  71.4 0.6 copy-start.2
